TPU v7x, 32 devices: a whole 2x2x4 slice. The times are simulated.
32 devices in a mesh: sec: 4 (over y, core), row: 8 (over z, x).
Axes of the slice: x: 2, y: 2, z: 4, core: 2. Of those that a mesh axis runs over, the one named last changes fastest.
Arguments:
- section_image: float32 [4, 128, 2048], P('sec', 'row'), may hold values from -6 to 6
- drift_offsets: int32 [4, 2], replicated, may hold values from -4 to 4, as said below
- stem_weight: float32 [28, 1, 5, 5], replicated, may hold values from -1.25 to 1.25
- stem_bias: float32 [28], replicated, may hold values from -3 to 3
- first_weight: bfloat16 [28, 28, 3, 3, 3], replicated, may hold values from -0.21875 to 0.21875
- first_bias: float32 [28], replicated, may hold values from -3 to 3
- second_weight: bfloat16 [28, 28, 3, 3, 3], replicated, may hold values from -0.21875 to 0.21875
- second_bias: float32 [28], replicated, may hold values from -3 to 3
Outputs:
- volume_out: bfloat16 [28, 4, 64, 1024], P(None, None, 'row', 'sec')
Inputs may be any that keep to these rules, and one draw needn't show every extreme that they name: `drift_offsets`: offsets lie within plus or minus 4.
All inputs are finite; a program needn't handle non-finite values.
Results may differ from a plain program's by a relative error of at most 0.0049.
Values may be sent and summed in bfloat16 or wider, within the bound.
A program may use at most 64 MiB of HBM per device.

v0:
```python
import functools

import jax
import jax.numpy as jnp
from jax import lax
from jax.experimental import pallas as pl
from jax.experimental.pallas import tpu as pltpu
from jax.sharding import PartitionSpec as P

CP = 32
KJ = 256
MESH = pl.DeviceIdType.MESH


def gather_kernel(n_sec, n_row, cols, img_ref, g_ref, planes, send_sem, recv_sem):
    sec, row = lax.axis_index("sec"), lax.axis_index("row")
    _, rows, width = img_ref.shape
    out_width = width // 2
    wide = cols + 256
    has = {-1: row > 0, 0: None, 1: row < n_row - 1}

    def partners(act):
        for d in (-1, 0, 1):

            def each(d=d):
                for k in range(n_sec):
                    if k or d:
                        act(d, k)

            if d:
                pl.when(has[d])(each)
            else:
                each()

    barrier = pltpu.get_barrier_semaphore()

    def greet(d, k):
        pl.semaphore_signal(
            barrier,
            inc=1,
            device_id=(lax.rem(sec + k, n_sec), row + d),
            device_id_type=MESH,
        )

    partners(greet)

    image = img_ref[0]
    high = image.astype(jnp.bfloat16)
    low = (image - high.astype(jnp.float32)).astype(jnp.bfloat16)
    chunks = width // 256
    stacked = jnp.concatenate(
        [part[:, c * 256 : (c + 1) * 256] for part in (high, low) for c in range(chunks)], axis=0
    )
    source = lax.broadcasted_iota(jnp.int32, (256, 256), 0)
    target = lax.broadcasted_iota(jnp.int32, (256, 256), 1)
    wanted = jnp.where(target < 128, 2 * target, 2 * target - 255)
    pick = jnp.where(source == wanted, 1.0, 0.0).astype(jnp.bfloat16)
    split = jnp.dot(stacked, pick, preferred_element_type=jnp.float32).astype(jnp.bfloat16)
    edge = jnp.zeros((4, rows, 128), jnp.bfloat16)
    planes[:, :, 0:128] = edge
    planes[:, :, 128 + out_width : 256 + out_width] = edge
    for part in range(2):
        for c in range(chunks):
            at = (part * chunks + c) * rows
            for odd in range(2):
                planes[2 * part + odd, :, 128 + c * 128 : 256 + c * 128] = split[
                    at : at + rows, odd * 128 : odd * 128 + 128
                ]

    @pl.when(row == 0)
    def _():
        g_ref[0] = jnp.zeros(g_ref.shape[1:], jnp.bfloat16)

    @pl.when(row == n_row - 1)
    def _():
        g_ref[2] = jnp.zeros(g_ref.shape[1:], jnp.bfloat16)

    up = jnp.where(row > 0, 1, 0)
    down = jnp.where(row < n_row - 1, 1, 0)
    pl.semaphore_wait(barrier, n_sec * (1 + up + down) - 1)

    def window(owner):
        return planes.at[:, :, pl.ds(pl.multiple_of(owner * cols, 128), wide)]

    def outgoing(d, k):
        owner = lax.rem(sec + k, n_sec)
        return pltpu.make_async_remote_copy(
            src_ref=window(owner),
            dst_ref=g_ref.at[1 - d, sec],
            send_sem=send_sem.at[1 - d, k],
            recv_sem=recv_sem.at[1 - d, k],
            device_id=(owner, row + d),
            device_id_type=MESH,
        )

    def incoming(d, k):
        origin = lax.rem(sec + n_sec - k, n_sec)
        return pltpu.make_async_remote_copy(
            src_ref=window(sec),
            dst_ref=g_ref.at[1 + d, origin],
            send_sem=send_sem.at[1 + d, k],
            recv_sem=recv_sem.at[1 + d, k],
            device_id=(origin, row + d),
            device_id_type=MESH,
        )

    partners(lambda d, k: outgoing(d, k).start())
    own = pltpu.make_async_copy(window(sec), g_ref.at[1, sec], send_sem.at[1, 0])
    own.start()
    own.wait()
    partners(lambda d, k: outgoing(d, k).wait_send())
    partners(lambda d, k: incoming(d, k).wait_recv())


def toeplitz(base, reps, step, out_ref):
    for r in range(reps):
        out_ref[r * CP : (r + 1) * CP, :] = (
            pltpu.roll(base, step * r, 1) if r else base
        ).astype(jnp.bfloat16)


def block_kernel(
    n_rows, n_cols, drift_ref, g_ref, stem_ref, b1_ref, b2_ref, bias_ref, out_ref, ts, t1, t2, x1, x2
):
    sec, row = lax.axis_index("sec"), lax.axis_index("row")
    _, sections, _, in_rows, wide = g_ref.shape
    channels, _, out_rows, cols = out_ref.shape
    lanes = cols + 128
    rows_a, rows_h = out_rows + 4, out_rows + 2
    seg1, seg2 = rows_a * CP, rows_h * CP
    high_rows = 3 * in_rows

    stem = stem_ref[...]
    for r in range(rows_a):
        rolled = pltpu.roll(stem, 2 * r, 1) if r else stem
        high = rolled.astype(jnp.bfloat16)
        low = (rolled - high.astype(jnp.float32)).astype(jnp.bfloat16)
        at = slice(r * CP, (r + 1) * CP)
        ts[at, 0:KJ] = high
        ts[at, KJ : 2 * KJ] = high
        ts[at, 2 * KJ : 3 * KJ] = low
    toeplitz(b1_ref[...].astype(jnp.float32), rows_h, CP, t1)
    toeplitz(b2_ref[...].astype(jnp.float32), out_rows, CP, t2)
    nothing = jnp.zeros((3 * seg1, lanes), jnp.bfloat16)
    x1[0 : 3 * seg1, :] = nothing
    x1[(sections + 1) * 3 * seg1 :, :] = nothing
    x2[0 : 3 * seg2, :] = nothing[: 3 * seg2]
    tail = x2.shape[0] - (sections + 1) * 3 * seg2
    x2[(sections + 1) * 3 * seg2 :, :] = nothing[:tail]

    def inside(first, size, limit, axis, repeat, shift=None):
        shape = (size * repeat, 1) if axis == 0 else (1, size)
        pos = lax.broadcasted_iota(jnp.int32, shape, axis)
        pos = (pos // repeat if repeat > 1 else pos) + first
        ok = (pos >= 0) & (pos < limit)
        if shift is not None:
            ok = ok & (pos + shift >= 0) & (pos + shift < limit)
        return jnp.where(ok, 1.0, 0.0)

    def column(which, reps):
        return jnp.concatenate([bias_ref[which, :, 0:1]] * reps, axis=0)

    def spread(value, ref, start, seg):
        for d in range(3):
            moved = pltpu.roll(value, lanes - d, 1) if d else value
            ref[pl.ds(pl.multiple_of(start + d * seg, CP), seg), :] = moved.astype(jnp.bfloat16)

    first_row, first_col = row * out_rows, sec * cols

    def stem_step(s, carry):
        dr, dc = drift_ref[s, 0], drift_ref[s, 1]
        taps = []
        for odd in range(2):
            plane = jnp.concatenate(
                [
                    g_ref[b, s, odd].astype(jnp.float32) + g_ref[b, s, 2 + odd].astype(jnp.float32)
                    for b in range(3)
                ],
                axis=0,
            )
            plane = pltpu.roll(plane, lax.rem(high_rows - 2 * dr, high_rows), 0)
            taps.append(pltpu.roll(plane, wide - 126 - dc, 1))
        even, odd = taps
        shifted = [
            pltpu.roll(even, 1, 1),
            pltpu.roll(odd, 1, 1),
            even,
            odd,
            pltpu.roll(even, wide - 1, 1),
        ]
        field = jnp.concatenate(
            [part[:, :lanes] for part in shifted]
            + [jnp.zeros((KJ - 5 * high_rows, lanes), jnp.float32)],
            axis=0,
        )
        high = field.astype(jnp.bfloat16)
        low = (field - high.astype(jnp.float32)).astype(jnp.bfloat16)
        result = jnp.dot(
            ts[...], jnp.concatenate([high, low, high], axis=0), preferred_element_type=jnp.float32
        )
        result = jnp.maximum(result + column(0, rows_a), 0.0)
        result = result * inside(first_row - 2, rows_a, n_rows, 0, CP, dr)
        result = result * inside(first_col - 2, lanes, n_cols, 1, 1, dc)
        spread(result, x1, (s + 1) * 3 * seg1, seg1)
        return carry

    lax.fori_loop(0, sections, stem_step, 0)

    def first_step(s, carry):
        at = pl.ds(pl.multiple_of(s * 3 * seg1, CP), t1.shape[1])
        result = jnp.dot(t1[...], x1[at, :], preferred_element_type=jnp.float32)
        result = jnp.maximum(result + column(1, rows_h), 0.0)
        result = result * inside(first_row - 1, rows_h, n_rows, 0, CP)
        result = result * inside(first_col - 1, lanes, n_cols, 1, 1)
        spread(result, x2, (s + 1) * 3 * seg2, seg2)
        return carry

    lax.fori_loop(0, sections, first_step, 0)

    def second_step(s, carry):
        at = pl.ds(pl.multiple_of(s * 3 * seg2, CP), t2.shape[1])
        result = jnp.dot(t2[...], x2[at, 0:cols], preferred_element_type=jnp.float32)
        start = (s + 1) * 3 * seg1 + 2 * seg1 + 2 * CP
        kept = x1[pl.ds(pl.multiple_of(start, CP), out_rows * CP), 0:cols]
        result = result + column(2, out_rows) + kept.astype(jnp.float32)
        result = jnp.swapaxes(result.reshape(out_rows, CP, cols), 0, 1)
        out_ref[:, pl.ds(s, 1)] = result[:channels, None].astype(jnp.bfloat16)
        return carry

    lax.fori_loop(0, sections, second_step, 0)


def conv_base(weight, rows, total):
    out, inner = weight.shape[:2]
    base = jnp.transpose(weight, (0, 2, 4, 3, 1))
    base = jnp.pad(base, ((0, CP - out), (0, 0), (0, 0), (0, rows - 3), (0, CP - inner)))
    base = base.reshape(CP, 9 * rows * CP)
    return jnp.pad(base, ((0, 0), (0, total - base.shape[1])))


def on_device(
    n_sec,
    n_row,
    section_image,
    drift_offsets,
    stem_weight,
    stem_bias,
    first_weight,
    first_bias,
    second_weight,
    second_bias,
):
    _, in_rows, width = section_image.shape
    sections = n_sec
    channels = stem_weight.shape[0]
    out_rows, out_width = in_rows // 2, width // 2
    cols = out_width // n_sec
    wide, lanes = cols + 256, cols + 128
    vmem = pl.BlockSpec(memory_space=pltpu.VMEM)
    gathered = pl.pallas_call(
        functools.partial(gather_kernel, n_sec, n_row, cols),
        out_shape=jax.ShapeDtypeStruct((3, sections, 4, in_rows, wide), jnp.bfloat16),
        in_specs=[vmem],
        out_specs=vmem,
        scratch_shapes=[
            pltpu.VMEM((4, in_rows, out_width + 256), jnp.bfloat16),
            pltpu.SemaphoreType.DMA((3, n_sec)),
            pltpu.SemaphoreType.DMA((3, n_sec)),
        ],
        compiler_params=pltpu.CompilerParams(collective_id=0, has_side_effects=True),
        name="gather_image",
    )(section_image)

    k1 = 9 * (out_rows + 4) * CP
    k2 = -(-9 * (out_rows + 2) * CP // 128) * 128
    stem = jnp.transpose(stem_weight[:, 0], (0, 2, 1))
    stem = jnp.pad(stem, ((0, CP - channels), (0, 0), (in_rows - 6, 2 * in_rows + 1)))
    stem = stem.reshape(CP, 15 * in_rows)
    stem = jnp.pad(stem, ((0, 0), (0, KJ - stem.shape[1])))
    biases = jnp.stack([stem_bias, first_bias, second_bias])
    biases = jnp.pad(biases, ((0, 0), (0, CP - channels)))
    biases = jnp.broadcast_to(biases[:, :, None], (3, CP, 128))
    seg1, seg2 = (out_rows + 4) * CP, (out_rows + 2) * CP
    return pl.pallas_call(
        functools.partial(block_kernel, n_row * out_rows, out_width),
        out_shape=jax.ShapeDtypeStruct((channels, sections, out_rows, cols), jnp.bfloat16),
        in_specs=[pl.BlockSpec(memory_space=pltpu.SMEM)] + [vmem] * 5,
        out_specs=vmem,
        scratch_shapes=[
            pltpu.VMEM((seg1, 3 * KJ), jnp.bfloat16),
            pltpu.VMEM((seg2, k1), jnp.bfloat16),
            pltpu.VMEM((out_rows * CP, k2), jnp.bfloat16),
            pltpu.VMEM(((sections + 2) * 3 * seg1, lanes), jnp.bfloat16),
            pltpu.VMEM(((sections + 2) * 3 * seg2 + k2 - 9 * seg2, lanes), jnp.bfloat16),
        ],
        compiler_params=pltpu.CompilerParams(vmem_limit_bytes=48 * 1024 * 1024),
        name="stem_and_block",
    )(
        drift_offsets,
        gathered,
        stem,
        conv_base(first_weight, out_rows + 4, k1),
        conv_base(second_weight, out_rows + 2, k2),
        biases,
    )


def solution(mesh):
    placed = (P("sec", "row", None), P(), P(), P(), P(), P(), P(), P())
    return jax.shard_map(
        functools.partial(on_device, mesh.shape["sec"], mesh.shape["row"]),
        mesh=mesh,
        in_specs=placed,
        out_specs=P(None, None, "row", "sec"),
        check_vma=False,
    )
```

profile of v0, /device:TPU:17, one launch (start us, length us, event | category | flops | bytes accessed | tf_op | source)
XLA Modules:
  0.0 37.4 jit_solution(8700902498154831999)
XLA Ops:
  0.0 1.1 %copy.20 = bf16[28,3,3,3,28]{4,3,2,1,0:T(4,128)(2,1)S(1)} copy(bf16[28,3,3,3,28]{4,0,2,3,1:T(8,128)(2,1)} %bitcast.10) | data formatting | bytes 84672
  1.1 0.2 pad.27.clone
  1.3 0.0 copy-start.1
  1.3 0.7 %reshape.12 = bf16[32,2880]{1,0:T(8,128)(2,1)S(1)} reshape(bf16[32,3,3,10,32]{4,3,2,1,0:T(8,128)(2,1)S(1)} %pad.27.clone) | data formatting | bytes 368640 | tf_op jit(solution)/shard_map/reshape | solution.py:237
  2.0 0.2 copy-done.1
  2.2 0.1 copy.19
  2.4 0.2 pad.26.clone
  2.6 0.0 copy-start.2
  2.6 0.0 copy-start.4
  2.6 0.0 copy-start.5
  2.6 0.0 copy-start.6
  2.6 0.0 copy-start.3
  2.6 0.8 %reshape.11.b1_ref = bf16[32,3456]{1,0:T(8,128)(2,1)S(1)} reshape(bf16[32,3,3,12,32]{4,3,2,1,0:T(8,128)(2,1)S(1)} %pad.26.clone) | data formatting | bytes 442368 | tf_op jit(solution)/shard_map/reshape | solution.py:237
  3.4 18.1 %gather_image.1.g_ref = bf16[3,4,4,16,512]{4,3,2,1,0:T(8,128)(2,1)} custom-call(f32[1,16,2048]{2,1,0:T(8,128)} %img_ref.1), custom_call_target="tpu_custom_call" | custom-call | tf_op jit(solution)/shard_map/gather_image/pallas_call | solution.py:260
  21.6 0.0 copy-done.2
  21.6 0.1 copy.21
  21.7 0.1 pad.24.clone
  21.8 0.1 reshape.10
  21.9 0.0 copy-done.4
  21.9 0.0 copy-done.5
  21.9 0.0 copy-done.6
  22.0 0.1 broadcast_in_dim.2.bias_ref
  22.0 0.0 copy-done.3
  22.0 0.1 copy.16.drift_ref
  22.1 0.0 copy-start
  22.1 1.1 %copy-done = bf16[3,4,4,16,512]{4,3,2,1,0:T(8,128)(2,1)S(1)} copy-done((bf16[3,4,4,16,512]{4,3,2,1,0:T(8,128)(2,1)S(1)}, bf16[3,4,4,16,512]{4,3,2,1,0:T(8,128)(2,1)}, u32[]{:S(2)}) %copy-start) | copy-done | bytes 786456
  23.3 14.1 %stem_and_block.1 = bf16[28,4,8,256]{3,2,1,0:T(8,128)(2,1)} custom-call(s32[4,2]{1,0:T(4,128)S(1)} %copy.16.drift_ref, bf16[3,4,4,16,512]{4,3,2,1,0:T(8,128)(2,1)S(1)} %copy-done, f32[32,256]{1,0:T(8,128)S(1)} %pad.25.stem_ref, bf16[32,3456]{1,0:T(8,128)(2,1)S(1)} %reshape.11.b1_ref, bf16[32,2944]{1,0:T(8,128)(2,1)S(1)} %pad.28.b2_ref, ...), custom_call_target="tpu_custom_call" | custom-call | tf_op jit(solution)/shard_map/stem_and_block/pallas_call | solution.py:284
  (3 shorter events, 0.0 us)
Async XLA Ops:
  1.3 0.9 %copy-start.1 = (bf16[28,28,3,3,3]{1,0,4,3,2:T(8,128)(2,1)S(1)}, bf16[28,28,3,3,3]{1,0,4,3,2:T(8,128)(2,1)}, u32[]{:S(2)}) copy-start(bf16[28,28,3,3,3]{1,0,4,3,2:T(8,128)(2,1)} %param.12) | copy-start | bytes 127012
  2.6 19.0 %copy-start.2 = (f32[28,1,5,5]{0,1,3,2:T(1,128)S(1)}, f32[28,1,5,5]{0,1,3,2:T(1,128)}, u32[]{:S(2)}) copy-start(f32[28,1,5,5]{0,1,3,2:T(1,128)} %param.10) | copy-start | bytes 8404
  2.6 19.3 %copy-start.4 = (f32[28]{0:T(128)S(1)}, f32[28]{0:T(128)}, u32[]{:S(2)}) copy-start(f32[28]{0:T(128)} %param.15) | copy-start | bytes 340
  2.6 19.3 %copy-start.5 = (f32[28]{0:T(128)S(1)}, f32[28]{0:T(128)}, u32[]{:S(2)}) copy-start(f32[28]{0:T(128)} %param.13) | copy-start | bytes 340
  2.6 19.3 %copy-start.6 = (f32[28]{0:T(128)S(1)}, f32[28]{0:T(128)}, u32[]{:S(2)}) copy-start(f32[28]{0:T(128)} %param.11) | copy-start | bytes 340
  2.6 19.4 %copy-start.3 = (s32[4,2]{0,1:T(2,128)S(1)}, s32[4,2]{0,1:T(2,128)}, u32[]{:S(2)}) copy-start(s32[4,2]{0,1:T(2,128)} %param.9) | copy-start | bytes 100
  22.1 1.1 %copy-start = (bf16[3,4,4,16,512]{4,3,2,1,0:T(8,128)(2,1)S(1)}, bf16[3,4,4,16,512]{4,3,2,1,0:T(8,128)(2,1)}, u32[]{:S(2)}) copy-start(bf16[3,4,4,16,512]{4,3,2,1,0:T(8,128)(2,1)} %gather_image.1.g_ref) | copy-start | bytes 2359300
where the time goes:
time: 37.6 us; the launch traced here: 37.4 us
  Pallas kernels  32.2 us (86%)
  local copies, waits for them, and re-layouts  4.97 us (13%)
    pallas_call x1, Pallas kernels, on_device(): pl.pallas_call(functools.partial(gather_kernel, n_sec, n_row, cols), out_...  18.1 us
    pallas_call x1, Pallas kernels, on_device(): pl.pallas_call(functools.partial(block_kernel, n_row * out_rows, out_widt...  14.1 us
    unnamed x17, local copies, waits for them, and re-layouts  2.71 us
    reshape x2, local copies, waits for them, and re-layouts, conv_base(): base = base.reshape(CP, 9 * rows * CP)  1.41 us

commit v1 on v0

--- a/solution.py
+++ b/solution.py
@@ -12,15 +12,26 @@
 MESH = pl.DeviceIdType.MESH
 
 
-def gather_kernel(n_sec, n_row, cols, img_ref, g_ref, planes, send_sem, recv_sem):
+def toeplitz(base, reps, step, out_ref):
+    for r in range(reps):
+        out_ref[r * CP : (r + 1) * CP, :] = (
+            pltpu.roll(base, step * r, 1) if r else base
+        ).astype(jnp.bfloat16)
+
+
+def kernel(
+    n_sec, n_row, drift_ref, img_ref, stem_ref, w1_ref, w2_ref, bias_ref, out_ref,
+    msg, g_ref, base, ts, t1, t2, x1, x2, send_sem, recv_sem, own_sem,
+):
     sec, row = lax.axis_index("sec"), lax.axis_index("row")
     _, rows, width = img_ref.shape
     out_width = width // 2
-    wide = cols + 256
+    n_rows, n_cols = n_row * rows // 2, out_width
+    cols = out_width // n_sec
     has = {-1: row > 0, 0: None, 1: row < n_row - 1}
 
     def partners(act):
-        for d in (-1, 0, 1):
+        for d in (-1, 1, 0):
 
             def each(d=d):
                 for k in range(n_sec):
@@ -55,17 +66,31 @@
     target = lax.broadcasted_iota(jnp.int32, (256, 256), 1)
     wanted = jnp.where(target < 128, 2 * target, 2 * target - 255)
     pick = jnp.where(source == wanted, 1.0, 0.0).astype(jnp.bfloat16)
-    split = jnp.dot(stacked, pick, preferred_element_type=jnp.float32).astype(jnp.bfloat16)
-    edge = jnp.zeros((4, rows, 128), jnp.bfloat16)
-    planes[:, :, 0:128] = edge
-    planes[:, :, 128 + out_width : 256 + out_width] = edge
-    for part in range(2):
-        for c in range(chunks):
-            at = (part * chunks + c) * rows
+    split = jnp.dot(stacked, pick, preferred_element_type=jnp.float32)
+
+    def piece(part, odd, c):
+        if c < 0 or c >= chunks:
+            return jnp.zeros((rows, 128), jnp.float32)
+        at = (part * chunks + c) * rows
+        return split[at : at + rows, odd * 128 : odd * 128 + 128]
+
+    lane = lax.broadcasted_iota(jnp.int32, (rows, 128), 1)
+    per = cols // 128
+    for q in range(n_sec):
+        edge = jnp.zeros((rows, 128), jnp.float32)
+        for part in range(2):
             for odd in range(2):
-                planes[2 * part + odd, :, 128 + c * 128 : 256 + c * 128] = split[
-                    at : at + rows, odd * 128 : odd * 128 + 128
-                ]
+                p = 2 * part + odd
+                for c in range(per):
+                    msg[q, p, :, c * 128 : (c + 1) * 128] = piece(part, odd, q * per + c).astype(
+                        jnp.bfloat16
+                    )
+                left, right = piece(part, odd, q * per - 1), piece(part, odd, (q + 1) * per)
+                both = jnp.where(lane >= 120, left, jnp.where(lane < 8, right, 0.0))
+                edge = edge + pltpu.roll(both, p * 16 + 8, 1)
+        msg[q, 4, :, 0:128] = edge.astype(jnp.bfloat16)
+        for c in range(1, per):
+            msg[q, 4, :, c * 128 : (c + 1) * 128] = jnp.zeros((rows, 128), jnp.bfloat16)
 
     @pl.when(row == 0)
     def _():
@@ -79,13 +104,10 @@
     down = jnp.where(row < n_row - 1, 1, 0)
     pl.semaphore_wait(barrier, n_sec * (1 + up + down) - 1)
 
-    def window(owner):
-        return planes.at[:, :, pl.ds(pl.multiple_of(owner * cols, 128), wide)]
-
     def outgoing(d, k):
         owner = lax.rem(sec + k, n_sec)
         return pltpu.make_async_remote_copy(
-            src_ref=window(owner),
+            src_ref=msg.at[owner],
             dst_ref=g_ref.at[1 - d, sec],
             send_sem=send_sem.at[1 - d, k],
             recv_sem=recv_sem.at[1 - d, k],
@@ -96,7 +118,7 @@
     def incoming(d, k):
         origin = lax.rem(sec + n_sec - k, n_sec)
         return pltpu.make_async_remote_copy(
-            src_ref=window(sec),
+            src_ref=msg.at[sec],
             dst_ref=g_ref.at[1 + d, origin],
             send_sem=send_sem.at[1 + d, k],
             recv_sem=recv_sem.at[1 + d, k],
@@ -105,26 +127,12 @@
         )
 
     partners(lambda d, k: outgoing(d, k).start())
-    own = pltpu.make_async_copy(window(sec), g_ref.at[1, sec], send_sem.at[1, 0])
+    own = pltpu.make_async_copy(msg.at[sec], g_ref.at[1, sec], own_sem)
     own.start()
-    own.wait()
-    partners(lambda d, k: outgoing(d, k).wait_send())
-    partners(lambda d, k: incoming(d, k).wait_recv())
-
-
-def toeplitz(base, reps, step, out_ref):
-    for r in range(reps):
-        out_ref[r * CP : (r + 1) * CP, :] = (
-            pltpu.roll(base, step * r, 1) if r else base
-        ).astype(jnp.bfloat16)
-
-
-def block_kernel(
-    n_rows, n_cols, drift_ref, g_ref, stem_ref, b1_ref, b2_ref, bias_ref, out_ref, ts, t1, t2, x1, x2
-):
-    sec, row = lax.axis_index("sec"), lax.axis_index("row")
-    _, sections, _, in_rows, wide = g_ref.shape
-    channels, _, out_rows, cols = out_ref.shape
+
+    _, sections, _, in_rows, _ = g_ref.shape
+    wide = cols + 256
+    channels, _, out_rows, _ = out_ref.shape
     lanes = cols + 128
     rows_a, rows_h = out_rows + 4, out_rows + 2
     seg1, seg2 = rows_a * CP, rows_h * CP
@@ -139,8 +147,14 @@
         ts[at, 0:KJ] = high
         ts[at, KJ : 2 * KJ] = high
         ts[at, 2 * KJ : 3 * KJ] = low
-    toeplitz(b1_ref[...].astype(jnp.float32), rows_h, CP, t1)
-    toeplitz(b2_ref[...].astype(jnp.float32), out_rows, CP, t2)
+    for w_ref, seg, reps, ref in ((w1_ref, seg1, rows_h, t1), (w2_ref, seg2, out_rows, t2)):
+        base[...] = jnp.zeros(base.shape, jnp.float32)
+        for ds in range(3):
+            for tap in range(3):
+                for dx in range(3):
+                    at = (ds * 3 + dx) * seg + tap * CP
+                    base[0:channels, at : at + channels] = w_ref[ds, tap, dx].astype(jnp.float32)
+        toeplitz(base[:, : ref.shape[1]], reps, CP, ref)
     nothing = jnp.zeros((3 * seg1, lanes), jnp.bfloat16)
     x1[0 : 3 * seg1, :] = nothing
     x1[(sections + 1) * 3 * seg1 :, :] = nothing
@@ -165,19 +179,25 @@
             moved = pltpu.roll(value, lanes - d, 1) if d else value
             ref[pl.ds(pl.multiple_of(start + d * seg, CP), seg), :] = moved.astype(jnp.bfloat16)
 
+    own.wait()
+    partners(lambda d, k: incoming(d, k).wait_recv())
     first_row, first_col = row * out_rows, sec * cols
 
     def stem_step(s, carry):
         dr, dc = drift_ref[s, 0], drift_ref[s, 1]
         taps = []
         for odd in range(2):
-            plane = jnp.concatenate(
-                [
-                    g_ref[b, s, odd].astype(jnp.float32) + g_ref[b, s, 2 + odd].astype(jnp.float32)
-                    for b in range(3)
-                ],
-                axis=0,
-            )
+            blocks = []
+            for b in range(3):
+                rim = g_ref[b, s, 4, :, 0:128].astype(jnp.float32)
+                total = None
+                for p in (odd, 2 + odd):
+                    ends = pltpu.roll(rim, 120 - 16 * p, 1)
+                    main = g_ref[b, s, p].astype(jnp.float32)
+                    part = jnp.concatenate([ends, main, ends], axis=1)
+                    total = part if total is None else total + part
+                blocks.append(total)
+            plane = jnp.concatenate(blocks, axis=0)
             plane = pltpu.roll(plane, lax.rem(high_rows - 2 * dr, high_rows), 0)
             taps.append(pltpu.roll(plane, wide - 126 - dc, 1))
         even, odd = taps
@@ -228,14 +248,7 @@
         return carry
 
     lax.fori_loop(0, sections, second_step, 0)
-
-
-def conv_base(weight, rows, total):
-    out, inner = weight.shape[:2]
-    base = jnp.transpose(weight, (0, 2, 4, 3, 1))
-    base = jnp.pad(base, ((0, CP - out), (0, 0), (0, 0), (0, rows - 3), (0, CP - inner)))
-    base = base.reshape(CP, 9 * rows * CP)
-    return jnp.pad(base, ((0, 0), (0, total - base.shape[1])))
+    partners(lambda d, k: outgoing(d, k).wait_send())
 
 
 def on_device(
@@ -255,22 +268,8 @@
     channels = stem_weight.shape[0]
     out_rows, out_width = in_rows // 2, width // 2
     cols = out_width // n_sec
-    wide, lanes = cols + 256, cols + 128
+    lanes = cols + 128
     vmem = pl.BlockSpec(memory_space=pltpu.VMEM)
-    gathered = pl.pallas_call(
-        functools.partial(gather_kernel, n_sec, n_row, cols),
-        out_shape=jax.ShapeDtypeStruct((3, sections, 4, in_rows, wide), jnp.bfloat16),
-        in_specs=[vmem],
-        out_specs=vmem,
-        scratch_shapes=[
-            pltpu.VMEM((4, in_rows, out_width + 256), jnp.bfloat16),
-            pltpu.SemaphoreType.DMA((3, n_sec)),
-            pltpu.SemaphoreType.DMA((3, n_sec)),
-        ],
-        compiler_params=pltpu.CompilerParams(collective_id=0, has_side_effects=True),
-        name="gather_image",
-    )(section_image)
-
     k1 = 9 * (out_rows + 4) * CP
     k2 = -(-9 * (out_rows + 2) * CP // 128) * 128
     stem = jnp.transpose(stem_weight[:, 0], (0, 2, 1))
@@ -282,25 +281,33 @@
     biases = jnp.broadcast_to(biases[:, :, None], (3, CP, 128))
     seg1, seg2 = (out_rows + 4) * CP, (out_rows + 2) * CP
     return pl.pallas_call(
-        functools.partial(block_kernel, n_row * out_rows, out_width),
+        functools.partial(kernel, n_sec, n_row),
         out_shape=jax.ShapeDtypeStruct((channels, sections, out_rows, cols), jnp.bfloat16),
         in_specs=[pl.BlockSpec(memory_space=pltpu.SMEM)] + [vmem] * 5,
         out_specs=vmem,
         scratch_shapes=[
+            pltpu.VMEM((n_sec, 5, in_rows, cols), jnp.bfloat16),
+            pltpu.VMEM((3, sections, 5, in_rows, cols), jnp.bfloat16),
+            pltpu.VMEM((CP, max(k1, k2)), jnp.float32),
             pltpu.VMEM((seg1, 3 * KJ), jnp.bfloat16),
             pltpu.VMEM((seg2, k1), jnp.bfloat16),
             pltpu.VMEM((out_rows * CP, k2), jnp.bfloat16),
             pltpu.VMEM(((sections + 2) * 3 * seg1, lanes), jnp.bfloat16),
             pltpu.VMEM(((sections + 2) * 3 * seg2 + k2 - 9 * seg2, lanes), jnp.bfloat16),
+            pltpu.SemaphoreType.DMA((3, n_sec)),
+            pltpu.SemaphoreType.DMA((3, n_sec)),
+            pltpu.SemaphoreType.DMA,
         ],
-        compiler_params=pltpu.CompilerParams(vmem_limit_bytes=48 * 1024 * 1024),
-        name="stem_and_block",
+        compiler_params=pltpu.CompilerParams(
+            collective_id=0, has_side_effects=True, vmem_limit_bytes=48 * 1024 * 1024
+        ),
+        name="section_block",
     )(
         drift_offsets,
-        gathered,
+        section_image,
         stem,
-        conv_base(first_weight, out_rows + 4, k1),
-        conv_base(second_weight, out_rows + 2, k2),
+        jnp.transpose(first_weight, (2, 3, 4, 0, 1)),
+        jnp.transpose(second_weight, (2, 3, 4, 0, 1)),
         biases,
     )
 

time: 37.6 us -> 29.2 us (0.78)
  Pallas kernels: 32.2 us -> 24.9 us
  local copies, waits for them, and re-layouts: 4.97 us -> 4 us
    pallas_call x2 -> x1, Pallas kernels: 32.2 us -> 24.9 us  [on_device(): pl.pallas_call(functools.partial(kernel, n_sec, n_row), out_shape=jax.Sha...]
    reshape x2 -> x0, local copies, waits for them, and re-layouts: 1.41 us -> none  [conv_base(): base = base.reshape(CP, 9 * rows * CP)]
    unnamed x17 -> x18, local copies, waits for them, and re-layouts: 2.71 us -> 3.6 us
    pad x3 -> x0, local copies, waits for them, and re-layouts: 0.44 us -> none  [the longest x2 0.42 us: conv_base(): jnp.pad(base, ((0, CP - out), (0, 0), (0, 0), (0, rows - 3), (0, CP - inn...]
where the time goes in v1:
time: 29.2 us; the launch traced here: 29 us
  Pallas kernels  24.9 us (85%)
  local copies, waits for them, and re-layouts  4 us (14%)
    pallas_call x1, Pallas kernels, on_device(): pl.pallas_call(functools.partial(kernel, n_sec, n_row), out_shape=jax.Sha...  24.9 us
    unnamed x18, local copies, waits for them, and re-layouts  3.6 us

profile of v1, /device:TPU:17, one launch (start us, length us, event | category | flops | bytes accessed | tf_op | source)
XLA Modules:
  0.0 29.0 jit_solution(9449029300585926816)
XLA Ops:
  0.0 0.0 copy-start.4
  0.0 0.7 %copy-done.4 = s32[4,2]{0,1:T(2,128)S(1)} copy-done((s32[4,2]{0,1:T(2,128)S(1)}, s32[4,2]{0,1:T(2,128)}, u32[]{:S(2)}) %copy-start.4) | copy-done | bytes 56
  0.7 0.0 copy-start.5
  0.7 0.0 copy-start.6
  0.7 0.0 copy-start.7
  0.7 0.1 copy.12.drift_ref
  0.8 0.6 %copy-done.5 = f32[28]{0:T(128)S(1)} copy-done((f32[28]{0:T(128)S(1)}, f32[28]{0:T(128)}, u32[]{:S(2)}) %copy-start.5) | copy-done | bytes 136
  1.3 0.0 copy-done.6
  1.4 0.0 copy-done.7
  1.4 0.0 copy-start.3
  1.4 0.1 broadcast_in_dim.2.bias_ref
  1.5 0.6 %copy-done.3 = f32[28,1,5,5]{0,1,3,2:T(1,128)S(1)} copy-done((f32[28,1,5,5]{0,1,3,2:T(1,128)S(1)}, f32[28,1,5,5]{0,1,3,2:T(1,128)}, u32[]{:S(2)}) %copy-start.3) | copy-done | bytes 2824
  2.1 0.0 copy-start.2
  2.1 0.1 copy.15
  2.2 0.0 copy-start
  2.3 0.0 copy-start.1
  2.3 0.1 pad.12.clone
  2.4 0.1 reshape.4
  2.5 0.5 %copy-done.2 = f32[1,16,2048]{2,1,0:T(8,128)S(1)} copy-done((f32[1,16,2048]{2,1,0:T(8,128)S(1)}, f32[1,16,2048]{2,1,0:T(8,128)}, u32[]{:S(2)}) %copy-start.2) | copy-done | bytes 131096
  3.0 0.2 copy-done
  3.2 0.1 copy-done.1
  3.3 24.9 %section_block.1 = bf16[28,4,8,256]{3,2,1,0:T(8,128)(2,1)S(1)} custom-call(s32[4,2]{1,0:T(4,128)S(1)} %copy.12.drift_ref, f32[1,16,2048]{2,1,0:T(8,128)S(1)} %copy-done.2, f32[32,256]{1,0:T(8,128)S(1)} %pad.13.stem_ref, bf16[3,3,3,28,28]{4,3,2,1,0:T(8,128)(2,1)S(1)} %bitcast.9, bf16[3,3,3,28,28]{4,3,2,1,0:T(8,128)(2,1)S(1)} %bitcast.10, ...), custom_call_target="tpu_custom_call" | custom-call | tf_op jit(solution)/shard_map/section_block/pallas_call | solution.py:283
  28.2 0.8 %copy.17 = bf16[28,4,8,256]{3,2,1,0:T(8,128)(2,1)} copy(bf16[28,4,8,256]{3,2,1,0:T(8,128)(2,1)S(1)} %section_block.1) | data formatting | bytes 917504
  (2 shorter events, 0.0 us)
Async XLA Ops:
  0.0 0.7 %copy-start.4 = (s32[4,2]{0,1:T(2,128)S(1)}, s32[4,2]{0,1:T(2,128)}, u32[]{:S(2)}) copy-start(s32[4,2]{0,1:T(2,128)} %param.9) | copy-start | bytes 100
  0.7 0.7 %copy-start.5 = (f32[28]{0:T(128)S(1)}, f32[28]{0:T(128)}, u32[]{:S(2)}) copy-start(f32[28]{0:T(128)} %param.15) | copy-start | bytes 340
  0.7 0.7 %copy-start.6 = (f32[28]{0:T(128)S(1)}, f32[28]{0:T(128)}, u32[]{:S(2)}) copy-start(f32[28]{0:T(128)} %param.13) | copy-start | bytes 340
  0.7 0.7 %copy-start.7 = (f32[28]{0:T(128)S(1)}, f32[28]{0:T(128)}, u32[]{:S(2)}) copy-start(f32[28]{0:T(128)} %param.11) | copy-start | bytes 340
  1.4 0.7 %copy-start.3 = (f32[28,1,5,5]{0,1,3,2:T(1,128)S(1)}, f32[28,1,5,5]{0,1,3,2:T(1,128)}, u32[]{:S(2)}) copy-start(f32[28,1,5,5]{0,1,3,2:T(1,128)} %param.10) | copy-start | bytes 8404
  2.1 0.9 %copy-start.2 = (f32[1,16,2048]{2,1,0:T(8,128)S(1)}, f32[1,16,2048]{2,1,0:T(8,128)}, u32[]{:S(2)}) copy-start(f32[1,16,2048]{2,1,0:T(8,128)} %img_ref.1) | copy-start | bytes 393220
  2.2 1.0 %copy-start = (bf16[28,28,3,3,3]{1,0,4,3,2:T(8,128)(2,1)S(1)}, bf16[28,28,3,3,3]{1,0,4,3,2:T(8,128)(2,1)}, u32[]{:S(2)}) copy-start(bf16[28,28,3,3,3]{1,0,4,3,2:T(8,128)(2,1)} %param.12) | copy-start | bytes 127012
  2.3 1.1 %copy-start.1 = (bf16[28,28,3,3,3]{1,0,4,3,2:T(8,128)(2,1)S(1)}, bf16[28,28,3,3,3]{1,0,4,3,2:T(8,128)(2,1)}, u32[]{:S(2)}) copy-start(bf16[28,28,3,3,3]{1,0,4,3,2:T(8,128)(2,1)} %param.14) | copy-start | bytes 127012

commit v2 on v1

--- a/solution.py
+++ b/solution.py
@@ -20,8 +20,9 @@
 
 
 def kernel(
-    n_sec, n_row, drift_ref, img_ref, stem_ref, w1_ref, w2_ref, bias_ref, out_ref,
-    msg, g_ref, base, ts, t1, t2, x1, x2, send_sem, recv_sem, own_sem,
+    n_sec, n_row, drift_ref, img_hbm, stem_hbm, w1_hbm, w2_hbm, sb_hbm, fb_hbm, cb_hbm, out_ref,
+    img_ref, stem_ref, w1_ref, w2_ref, bias_rows, bias_ref,
+    msg, g_ref, base, ts, t1, t2, x1, x2, send_sem, recv_sem, own_sem, in_sem,
 ):
     sec, row = lax.axis_index("sec"), lax.axis_index("row")
     _, rows, width = img_ref.shape
@@ -31,18 +32,29 @@
     has = {-1: row > 0, 0: None, 1: row < n_row - 1}
 
     def partners(act):
-        for d in (-1, 1, 0):
-
-            def each(d=d):
-                for k in range(n_sec):
-                    if k or d:
-                        act(d, k)
-
-            if d:
-                pl.when(has[d])(each)
-            else:
-                each()
-
+        for k in range(n_sec):
+            for d in (-1, 1, 0):
+                if d:
+                    pl.when(has[d])(functools.partial(act, d, k))
+                elif k:
+                    act(d, k)
+
+    loads = [
+        pltpu.make_async_copy(source, target, in_sem.at[i])
+        for i, (source, target) in enumerate(
+            (
+                (img_hbm, img_ref),
+                (stem_hbm, stem_ref),
+                (sb_hbm, bias_rows.at[0]),
+                (fb_hbm, bias_rows.at[1]),
+                (cb_hbm, bias_rows.at[2]),
+                (w1_hbm, w1_ref),
+                (w2_hbm, w2_ref),
+            )
+        )
+    ]
+    for load in loads:
+        load.start()
     barrier = pltpu.get_barrier_semaphore()
 
     def greet(d, k):
@@ -55,6 +67,7 @@
 
     partners(greet)
 
+    loads[0].wait()
     image = img_ref[0]
     high = image.astype(jnp.bfloat16)
     low = (image - high.astype(jnp.float32)).astype(jnp.bfloat16)
@@ -138,7 +151,29 @@
     seg1, seg2 = rows_a * CP, rows_h * CP
     high_rows = 3 * in_rows
 
-    stem = stem_ref[...]
+    for load in loads[1:]:
+        load.wait()
+    parts = [stem_ref[i, j] for i in range(5) for j in range(5)] + [bias_rows[b] for b in range(3)]
+    parts.append(jnp.zeros((4, channels), jnp.float32))
+    small = jnp.concatenate(parts, axis=0)
+    item = lax.broadcasted_iota(jnp.int32, (32, KJ + 384), 0)
+    place = lax.broadcasted_iota(jnp.int32, (32, KJ + 384), 1)
+    tap_i, tap_j = item // 5, item % 5
+    spot = tap_j * high_rows + in_rows - 6 + tap_i
+    hit = ((item < 25) & (place < KJ) & (place == spot)) | (
+        (item >= 25) & (place >= KJ) & ((place - KJ) // 128 == item - 25)
+    )
+    laid = lax.dot_general(
+        small,
+        jnp.where(hit, 1.0, 0.0),
+        (((0,), (0,)), ((), ())),
+        precision=lax.Precision.HIGHEST,
+        preferred_element_type=jnp.float32,
+    )
+    laid = jnp.concatenate([laid, jnp.zeros((CP - channels, KJ + 384), jnp.float32)], axis=0)
+    stem = laid[:, :KJ]
+    for b in range(3):
+        bias_ref[b] = laid[:, KJ + b * 128 : KJ + (b + 1) * 128]
     for r in range(rows_a):
         rolled = pltpu.roll(stem, 2 * r, 1) if r else stem
         high = rolled.astype(jnp.bfloat16)
@@ -180,11 +215,13 @@
             ref[pl.ds(pl.multiple_of(start + d * seg, CP), seg), :] = moved.astype(jnp.bfloat16)
 
     own.wait()
-    partners(lambda d, k: incoming(d, k).wait_recv())
     first_row, first_col = row * out_rows, sec * cols
 
-    def stem_step(s, carry):
-        dr, dc = drift_ref[s, 0], drift_ref[s, 1]
+    def stem_step(k, carry):
+        s = lax.rem(sec + n_sec - k, n_sec)
+        for d, there in ((-1, has[-1]), (1, has[1]), (0, k > 0)):
+            pl.when(there)(lambda d=d: incoming(d, k).wait_recv())
+        dr, dc = drift_ref[0, s], drift_ref[1, s]
         taps = []
         for odd in range(2):
             blocks = []
@@ -272,20 +309,19 @@
     vmem = pl.BlockSpec(memory_space=pltpu.VMEM)
     k1 = 9 * (out_rows + 4) * CP
     k2 = -(-9 * (out_rows + 2) * CP // 128) * 128
-    stem = jnp.transpose(stem_weight[:, 0], (0, 2, 1))
-    stem = jnp.pad(stem, ((0, CP - channels), (0, 0), (in_rows - 6, 2 * in_rows + 1)))
-    stem = stem.reshape(CP, 15 * in_rows)
-    stem = jnp.pad(stem, ((0, 0), (0, KJ - stem.shape[1])))
-    biases = jnp.stack([stem_bias, first_bias, second_bias])
-    biases = jnp.pad(biases, ((0, 0), (0, CP - channels)))
-    biases = jnp.broadcast_to(biases[:, :, None], (3, CP, 128))
     seg1, seg2 = (out_rows + 4) * CP, (out_rows + 2) * CP
     return pl.pallas_call(
         functools.partial(kernel, n_sec, n_row),
         out_shape=jax.ShapeDtypeStruct((channels, sections, out_rows, cols), jnp.bfloat16),
-        in_specs=[pl.BlockSpec(memory_space=pltpu.SMEM)] + [vmem] * 5,
+        in_specs=[pl.BlockSpec(memory_space=pltpu.SMEM)] + [pl.BlockSpec(memory_space=pltpu.HBM)] * 7,
         out_specs=vmem,
         scratch_shapes=[
+            pltpu.VMEM(section_image.shape, jnp.float32),
+            pltpu.VMEM((5, 5, 1, channels), jnp.float32),
+            pltpu.VMEM((3, 3, 3, channels, channels), jnp.bfloat16),
+            pltpu.VMEM((3, 3, 3, channels, channels), jnp.bfloat16),
+            pltpu.VMEM((3, 1, channels), jnp.float32),
+            pltpu.VMEM((3, CP, 128), jnp.float32),
             pltpu.VMEM((n_sec, 5, in_rows, cols), jnp.bfloat16),
             pltpu.VMEM((3, sections, 5, in_rows, cols), jnp.bfloat16),
             pltpu.VMEM((CP, max(k1, k2)), jnp.float32),
@@ -297,18 +333,21 @@
             pltpu.SemaphoreType.DMA((3, n_sec)),
             pltpu.SemaphoreType.DMA((3, n_sec)),
             pltpu.SemaphoreType.DMA,
+            pltpu.SemaphoreType.DMA((7,)),
         ],
         compiler_params=pltpu.CompilerParams(
-            collective_id=0, has_side_effects=True, vmem_limit_bytes=48 * 1024 * 1024
+            collective_id=0, has_side_effects=True, vmem_limit_bytes=60 * 1024 * 1024
         ),
         name="section_block",
     )(
-        drift_offsets,
+        drift_offsets.T,
         section_image,
-        stem,
+        jnp.transpose(stem_weight, (2, 3, 1, 0)),
         jnp.transpose(first_weight, (2, 3, 4, 0, 1)),
         jnp.transpose(second_weight, (2, 3, 4, 0, 1)),
-        biases,
+        stem_bias[None],
+        first_bias[None],
+        second_bias[None],
     )
 
 

time: 29.2 us -> 25.6 us (0.88)
  local copies, waits for them, and re-layouts: 4 us -> 1.82 us
  Pallas kernels: 24.9 us -> 23.6 us
    unnamed x18 -> x1, local copies, waits for them, and re-layouts: 3.6 us -> 1.82 us
    pallas_call x1, Pallas kernels: 24.9 us -> 23.6 us  [on_device(): pl.pallas_call(functools.partial(kernel, n_sec, n_row), out_shape=jax.Sha...]
where the time goes in v2:
time: 25.6 us; the launch traced here: 25.4 us
  Pallas kernels  23.6 us (92%)
  local copies, waits for them, and re-layouts  1.82 us (7%)
    pallas_call x1, Pallas kernels, on_device(): pl.pallas_call(functools.partial(kernel, n_sec, n_row), out_shape=jax.Sha...  23.6 us
    unnamed x1, local copies, waits for them, and re-layouts  1.82 us

profile of v2, /device:TPU:17, one launch (start us, length us, event | category | flops | bytes accessed | tf_op | source)
XLA Modules:
  0.0 25.4 jit_solution(12117844372894344257)
XLA Ops:
  0.0 23.6 %section_block.1 = bf16[28,4,8,256]{3,2,1,0:T(8,128)(2,1)} custom-call(s32[2,4]{1,0:T(2,128)} %bitcast.10, f32[1,16,2048]{2,1,0:T(8,128)} %img_hbm.1, f32[5,5,1,28]{3,2,1,0:T(1,128)} %bitcast.9, bf16[3,3,3,28,28]{4,3,2,1,0:T(8,128)(2,1)} %bitcast.7, bf16[3,3,3,28,28]{4,3,2,1,0:T(8,128)(2,1)} %bitcast.8, f32[1,28]{1,0:T(1,128)} %bitcast.11, ...), custom_call_target="tpu_custom_call" | custom-call | tf_op jit(solution)/shard_map/section_block/pallas_call | solution.py:313
  23.6 1.8 %copy.10 = bf16[28,4,8,256]{3,2,1,0:T(8,128)(2,1)} copy(bf16[28,4,8,256]{3,2,1,0:T(8,128)(2,1)} %section_block.1) | data formatting | bytes 917504

commit v3 on v2

--- a/solution.py
+++ b/solution.py
@@ -312,7 +312,7 @@
     seg1, seg2 = (out_rows + 4) * CP, (out_rows + 2) * CP
     return pl.pallas_call(
         functools.partial(kernel, n_sec, n_row),
-        out_shape=jax.ShapeDtypeStruct((channels, sections, out_rows, cols), jnp.bfloat16),
+        out_shape=pltpu.VMEM((channels, sections, out_rows, cols), jnp.bfloat16),
         in_specs=[pl.BlockSpec(memory_space=pltpu.SMEM)] + [pl.BlockSpec(memory_space=pltpu.HBM)] * 7,
         out_specs=vmem,
         scratch_shapes=[

time: 25.6 us -> 23.7 us (0.926)
  local copies, waits for them, and re-layouts: 1.82 us -> 0.77 us
  Pallas kernels: 23.6 us -> 22.8 us
    unnamed x1, local copies, waits for them, and re-layouts: 1.82 us -> 0.77 us
    pallas_call x1, Pallas kernels: 23.6 us -> 22.8 us  [on_device(): pl.pallas_call(functools.partial(kernel, n_sec, n_row), out_shape=pltpu.V...]
where the time goes in v3:
time: 23.7 us; the launch traced here: 23.6 us
  Pallas kernels  22.8 us (96%)
  local copies, waits for them, and re-layouts  0.77 us (3%)
    pallas_call x1, Pallas kernels, on_device(): pl.pallas_call(functools.partial(kernel, n_sec, n_row), out_shape=pltpu.V...  22.8 us
    unnamed x1, local copies, waits for them, and re-layouts  0.77 us

profile of v3, /device:TPU:17, one launch (start us, length us, event | category | flops | bytes accessed | tf_op | source)
XLA Modules:
  0.0 23.6 jit_solution(13543226876683391067)
XLA Ops:
  0.0 22.8 %section_block.1 = bf16[28,4,8,256]{3,2,1,0:T(8,128)(2,1)S(1)} custom-call(s32[2,4]{1,0:T(2,128)} %bitcast.10, f32[1,16,2048]{2,1,0:T(8,128)} %img_hbm.1, f32[5,5,1,28]{3,2,1,0:T(1,128)} %bitcast.9, bf16[3,3,3,28,28]{4,3,2,1,0:T(8,128)(2,1)} %bitcast.7, bf16[3,3,3,28,28]{4,3,2,1,0:T(8,128)(2,1)} %bitcast.8, f32[1,28]{1,0:T(1,128)} %bitcast.11, ...), custom_call_target="tpu_custom_call" | custom-call | tf_op jit(solution)/shard_map/section_block/pallas_call | solution.py:313
  22.8 0.8 %copy.10 = bf16[28,4,8,256]{3,2,1,0:T(8,128)(2,1)} copy(bf16[28,4,8,256]{3,2,1,0:T(8,128)(2,1)S(1)} %section_block.1) | data formatting | bytes 917504

commit v4 on v3

--- a/solution.py
+++ b/solution.py
@@ -95,15 +95,14 @@
             for odd in range(2):
                 p = 2 * part + odd
                 for c in range(per):
-                    msg[q, p, :, c * 128 : (c + 1) * 128] = piece(part, odd, q * per + c).astype(
+                    at = p * cols + c * 128
+                    msg[q, :, at : at + 128] = piece(part, odd, q * per + c).astype(
                         jnp.bfloat16
                     )
                 left, right = piece(part, odd, q * per - 1), piece(part, odd, (q + 1) * per)
                 both = jnp.where(lane >= 120, left, jnp.where(lane < 8, right, 0.0))
                 edge = edge + pltpu.roll(both, p * 16 + 8, 1)
-        msg[q, 4, :, 0:128] = edge.astype(jnp.bfloat16)
-        for c in range(1, per):
-            msg[q, 4, :, c * 128 : (c + 1) * 128] = jnp.zeros((rows, 128), jnp.bfloat16)
+        msg[q, :, 4 * cols : 4 * cols + 128] = edge.astype(jnp.bfloat16)
 
     @pl.when(row == 0)
     def _():
@@ -143,7 +142,7 @@
     own = pltpu.make_async_copy(msg.at[sec], g_ref.at[1, sec], own_sem)
     own.start()
 
-    _, sections, _, in_rows, _ = g_ref.shape
+    _, sections, in_rows, _ = g_ref.shape
     wide = cols + 256
     channels, _, out_rows, _ = out_ref.shape
     lanes = cols + 128
@@ -226,11 +225,11 @@
         for odd in range(2):
             blocks = []
             for b in range(3):
-                rim = g_ref[b, s, 4, :, 0:128].astype(jnp.float32)
+                rim = g_ref[b, s, :, 4 * cols : 4 * cols + 128].astype(jnp.float32)
                 total = None
                 for p in (odd, 2 + odd):
                     ends = pltpu.roll(rim, 120 - 16 * p, 1)
-                    main = g_ref[b, s, p].astype(jnp.float32)
+                    main = g_ref[b, s, :, p * cols : (p + 1) * cols].astype(jnp.float32)
                     part = jnp.concatenate([ends, main, ends], axis=1)
                     total = part if total is None else total + part
                 blocks.append(total)
@@ -322,8 +321,8 @@
             pltpu.VMEM((3, 3, 3, channels, channels), jnp.bfloat16),
             pltpu.VMEM((3, 1, channels), jnp.float32),
             pltpu.VMEM((3, CP, 128), jnp.float32),
-            pltpu.VMEM((n_sec, 5, in_rows, cols), jnp.bfloat16),
-            pltpu.VMEM((3, sections, 5, in_rows, cols), jnp.bfloat16),
+            pltpu.VMEM((n_sec, in_rows, 4 * cols + 128), jnp.bfloat16),
+            pltpu.VMEM((3, sections, in_rows, 4 * cols + 128), jnp.bfloat16),
             pltpu.VMEM((CP, max(k1, k2)), jnp.float32),
             pltpu.VMEM((seg1, 3 * KJ), jnp.bfloat16),
             pltpu.VMEM((seg2, k1), jnp.bfloat16),

time: 23.7 us -> 23.2 us (0.979)
  Pallas kernels: 22.8 us -> 22.3 us
    pallas_call x1, Pallas kernels: 22.8 us -> 22.3 us  [on_device(): pl.pallas_call(functools.partial(kernel, n_sec, n_row), out_shape=pltpu.V...]
where the time goes in v4:
time: 23.2 us; the launch traced here: 23.1 us
  Pallas kernels  22.3 us (96%)
  local copies, waits for them, and re-layouts  0.77 us (3%)
    pallas_call x1, Pallas kernels, on_device(): pl.pallas_call(functools.partial(kernel, n_sec, n_row), out_shape=pltpu.V...  22.3 us
    unnamed x1, local copies, waits for them, and re-layouts  0.77 us

profile of v4, /device:TPU:17, one launch (start us, length us, event | category | flops | bytes accessed | tf_op | source)
XLA Modules:
  0.0 23.1 jit_solution(2542690704907402201)
XLA Ops:
  0.0 22.3 %section_block.1 = bf16[28,4,8,256]{3,2,1,0:T(8,128)(2,1)S(1)} custom-call(s32[2,4]{1,0:T(2,128)} %bitcast.10, f32[1,16,2048]{2,1,0:T(8,128)} %img_hbm.1, f32[5,5,1,28]{3,2,1,0:T(1,128)} %bitcast.9, bf16[3,3,3,28,28]{4,3,2,1,0:T(8,128)(2,1)} %bitcast.7, bf16[3,3,3,28,28]{4,3,2,1,0:T(8,128)(2,1)} %bitcast.8, f32[1,28]{1,0:T(1,128)} %bitcast.11, ...), custom_call_target="tpu_custom_call" | custom-call | tf_op jit(solution)/shard_map/section_block/pallas_call | solution.py:312
  22.3 0.8 %copy.10 = bf16[28,4,8,256]{3,2,1,0:T(8,128)(2,1)} copy(bf16[28,4,8,256]{3,2,1,0:T(8,128)(2,1)S(1)} %section_block.1) | data formatting | bytes 917504
